TPU v7x, 512 devices: a whole 4x8x8 slice. The times are simulated.
512 devices in a mesh: img: 8 (over y_lo, core), cin: 8 (over x, y_hi), cout: 8 (over z).
Axes of the slice: x: 4, y: 8 (y_hi: 2, y_lo: 4; y = y_hi * 4 + y_lo), z: 8, core: 2. Of those that a mesh axis runs over, the one named last changes fastest.
Arguments:
- maps: bfloat16 [2, 8, 14, 14, 1024], P(None, 'img'), may hold values from -6 to 6
- w_first: bfloat16 [3, 3, 1024, 1024], P(None, None, 'cin', 'cout'), may hold values from -0.09375 to 0.09375
- w_reduce: bfloat16 [3, 3, 1024, 8192], P(None, None, 'img', ('cin', 'cout')), may hold values from -0.09375 to 0.09375
- w_wide: bfloat16 [3, 3, 8192, 8192], P(None, None, 'cin', ('img', 'cout')), may hold values from -0.03125 to 0.03125
Outputs:
- wide_out: bfloat16 [2, 8, 7, 7, 8192], P(None, 'cin', None, None, ('img', 'cout'))
All inputs are finite; a program needn't handle non-finite values.
Results may differ from a plain program's by a relative error of at most 0.014.
Values may be sent and summed in bfloat16 or wider, within the bound.
No kernel may reach another device: no remote copies, remote signals or barrier semaphores. Data moves between devices by JAX's collectives and lax.ppermute only.
A program may use at most 64 MiB of HBM per device.

v0:
```python
import jax
import jax.numpy as jnp
from jax import lax
from jax.sharding import PartitionSpec as P


def conv_block(padded, weight_flat, size, step):
    channels = padded.shape[3]
    windows = []
    for row_tap in range(3):
        for col_tap in range(3):
            windows.append(
                padded[
                    :,
                    row_tap : row_tap + step * (size - 1) + 1 : step,
                    col_tap : col_tap + step * (size - 1) + 1 : step,
                    :,
                ]
            )
    table = jnp.concatenate(windows, axis=3).reshape(-1, 9 * channels)
    total = jnp.dot(table, weight_flat, preferred_element_type=jnp.float32)
    return total.reshape(padded.shape[0], size, size, weight_flat.shape[1])


def conv_taps(padded, weight, size, step):
    count = padded.shape[0]
    channels = padded.shape[3]
    weight_flat = weight.reshape(9 * channels, weight.shape[3])
    group = 1
    for trial in range(1, 9):
        if count % trial == 0:
            group = trial
    blocks = padded.reshape(count // group, group, padded.shape[1], padded.shape[2], channels)
    results = lax.map(lambda block: conv_block(block, weight_flat, size, step), blocks)
    return results.reshape(count, size, size, weight.shape[3])


def pad_map(values):
    return jnp.pad(values, ((0, 0), (1, 1), (1, 1), (0, 0)))


def local(maps, w_first, w_reduce, w_wide):
    batches = maps.shape[0]
    side = maps.shape[2]
    half = side // 2
    in_block = w_first.shape[2]
    out_block = w_first.shape[3]
    flat = maps.reshape(-1, side, side, maps.shape[4])
    in_part = lax.dynamic_slice_in_dim(flat, lax.axis_index("cin") * in_block, in_block, 3)
    first_terms = conv_taps(pad_map(jnp.maximum(in_part, 0)), w_first, side, 1)
    first_terms = first_terms.reshape(batches, maps.shape[1], side, side, out_block)
    summed = lax.psum(first_terms, "cin")
    own_part = lax.dynamic_slice_in_dim(maps, lax.axis_index("cout") * out_block, out_block, 4)
    segment_maps = (own_part.astype(jnp.float32) + summed).astype(jnp.bfloat16)
    whole = lax.all_gather(segment_maps, "cout", axis=4, tiled=True)
    by_channel = lax.all_to_all(whole, "img", split_axis=4, concat_axis=1, tiled=True)
    images = by_channel.shape[1]
    rect_segment = jnp.maximum(by_channel, 0).reshape(-1, side, side, by_channel.shape[4])
    reduced = conv_taps(pad_map(rect_segment), w_reduce, half, 2).reshape(
        batches, images, half, half, w_reduce.shape[3]
    )
    out_width = w_wide.shape[3]
    summed_wide = lax.psum(reduced, "img")
    narrow = jnp.maximum(summed_wide, 0.0).astype(jnp.bfloat16)
    gathered = lax.all_gather(narrow, "cout", axis=4, tiled=True)
    flat_all = gathered.reshape(-1, half, half, gathered.shape[4])
    partial_value = conv_taps(pad_map(flat_all), w_wide, half, 1)
    partial_value = partial_value.reshape(batches, images, half, half, out_width)
    result = lax.psum_scatter(
        partial_value.astype(jnp.bfloat16), "cin", scatter_dimension=1, tiled=True
    )
    return result


def solution(mesh):
    in_specs = (
        P(None, "img", None, None, None),
        P(None, None, "cin", "cout"),
        P(None, None, "img", ("cin", "cout")),
        P(None, None, "cin", ("img", "cout")),
    )
    out_specs = P(None, "cin", None, None, ("img", "cout"))
    return jax.shard_map(local, mesh=mesh, in_specs=in_specs, out_specs=out_specs, check_vma=False)
```

profile of v0, /device:TPU:64, one launch (start us, length us, event | category | flops | bytes accessed | tf_op | source)
XLA Modules:
  0.0 461.7 jit_solution(14591765025077755233)
XLA Ops:
  9.3 116.6 %all-reduce.8.cloned.1.call-done = f32[2,1,14,14,128]{4,3,2,0,1:T(8,128)} async-done(((f32[2,1,14,14,128]{4,3,2,0,1:T(8,128)}), f32[2,1,14,14,128]{4,3,2,0,1:T(8,128)}) %all-reduce.8.cloned.1.call-update) | async-done | bytes 200720 | tf_op jit(solution)/shard_map/psum | solution.py:52
  126.9 26.5 %all_gather.6 = bf16[2,1,14,14,1024]{4,3,2,0,1:T(8,128)(2,1)S(1)} all-gather(bf16[2,1,14,14,128]{4,3,2,0,1:T(8,128)(2,1)S(1)} %add_convert_fusion), channel_id=1, replica_groups=mesh['img'=8,'cin'=8,'cout'=8] {'cout'}, dimensions={4}, use_global_device_ids=true | all-gather | bytes 903168 | tf_op jit(solution)/shard_map/all_gather | solution.py:55
  153.5 12.4 %copy.42 = bf16[2,1,14,14,1024]{3,0,2,1,4:T(2,128)(2,1)} copy(bf16[2,1,14,14,1024]{4,3,2,0,1:T(8,128)(2,1)S(1)} %all_gather.6) | data formatting | bytes 1605632 | tf_op jit(solution)/shard_map/all_gather | solution.py:55
  165.8 12.8 %reshape.68 = bf16[8,2,25088]{2,1,0:T(2,128)(2,1)} reshape(bf16[1024,1,14,2,14]{4,3,2,1,0:T(2,128)(2,1)} %bitcast.84) | data formatting | bytes 1605632
  178.7 3.5 all-to-all-start
  182.3 21.2 %all-to-all-done = bf16[8,2,25088]{2,1,0:T(2,128)(2,1)S(1)} async-done(((bf16[8,2,25088]{2,1,0:T(2,128)(2,1)}), bf16[8,2,25088]{2,1,0:T(2,128)(2,1)S(1)}, u32[]{:S(2)}, u32[]{:S(2)}) %all-to-all-start) | async-done | bytes 802848 | tf_op jit(solution)/shard_map/all_to_all | solution.py:56
  203.4 19.8 %reshape.69 = bf16[1024,1,14,2,14]{4,3,2,1,0:T(2,128)(2,1)} reshape(bf16[8,2,25088]{2,1,0:T(2,128)(2,1)S(1)} %all-to-all-done) | data formatting | bytes 1605632
  223.2 17.3 %copy.43 = bf16[2,1,14,14,1024]{4,0,3,2,1:T(2,128)(2,1)S(1)} copy(bf16[2,1,14,14,1024]{3,0,2,1,4:T(2,128)(2,1)} %bitcast.85) | data formatting | bytes 1605632 | tf_op jit(solution)/shard_map/all_to_all | solution.py:56
  241.7 1.2 pad_bitcast_fusion.1
  242.9 4.0 while.26
  242.9 1.2 dynamic-slice_bitcast_fusion.6
  246.9 31.9 %all-reduce.11 = bf16[2,8,7,7,128]{4,1,0,3,2:T(8,128)(2,1)S(1)} all-reduce(f32[2,8,7,7,128]{4,1,0,3,2:T(8,128)S(1)} %get-tuple-element.61), channel_id=1, replica_groups=mesh['img'=8,'cin'=8,'cout'=8] {'img'}, use_global_device_ids=true, to_apply=%region_3.4 | all-reduce | flops 100352 | bytes 602112 | tf_op jit(solution)/shard_map/psum | solution.py:63
  279.6 41.6 %all-gather.2.cloned.1.call-done = bf16[2,8,7,7,1024]{4,1,0,3,2:T(8,128)(2,1)} async-done(((bf16[2,8,7,7,128]{4,1,0,3,2:T(8,128)(2,1)}), bf16[2,8,7,7,1024]{4,1,0,3,2:T(8,128)(2,1)}) %all-gather.2.cloned.1.call-update) | async-done | bytes 1605648 | tf_op jit(solution)/shard_map/all_gather | solution.py:65
  321.2 3.3 pad_bitcast_fusion
  324.5 17.2 %while.27 = (s32[]{:T(128)}, bf16[2,8,7,7,128]{4,0,3,2,1:T(2,128)(2,1)S(1)}, bf16[2,8,9,9,1024]{4,1,0,3,2:T(8,128)(2,1)}, bf16[9216,128]{1,0:T(8,128)(2,1)S(1)}) while((s32[]{:T(128)}, bf16[2,8,7,7,128]{4,0,3,2,1:T(2,128)(2,1)S(1)}, bf16[2,8,9,9,1024]{4,1,0,3,2:T(8,128)(2,1)}, bf16[9216,128]{1,0:T(8,128)(2,1)S(1)}) %tuple.60), condition=%wide.region_5.6_spmd.clone, body=%wide.region_4.5_spmd.sunk.clone | while | flops 924844032 | bytes 27191356 | solution.py:34
  324.5 1.4 dynamic-slice_bitcast_fusion.7
  326.5 2.0 fusion.29
  328.7 4.4 dynamic_update_slice.16
  333.1 1.4 dynamic-slice_bitcast_fusion.7
  335.1 2.0 fusion.29
  337.3 4.4 dynamic_update_slice.16
  342.5 1.3 dynamic-slice.2
  343.7 109.5 %all-reduce.10.cloned.1.call-done = bf16[2,8,7,7,128]{4,0,3,2,1:T(2,128)(2,1)} async-done(((bf16[2,8,7,7,128]{4,0,3,2,1:T(2,128)(2,1)}), bf16[2,8,7,7,128]{4,0,3,2,1:T(2,128)(2,1)}) %all-reduce.10.cloned.1.call-update) | async-done | bytes 200720
  453.3 1.9 constant_dynamic-slice_fusion
  (73 shorter events, 10.3 us)
Async XLA Ops:
  6.5 1.6 copy-start
  6.5 119.4 %all-reduce.8.cloned.1.call-start = ((), (), s32[]{:S(2)}) async-start(), calls=%async_computation.1 | async-start | bytes 458752 | tf_op jit(solution)/shard_map/psum | solution.py:52
  178.7 24.8 %all-to-all-start = ((bf16[8,2,25088]{2,1,0:T(2,128)(2,1)}), bf16[8,2,25088]{2,1,0:T(2,128)(2,1)S(1)}, u32[]{:S(2)}, u32[]{:S(2)}) async-start(bf16[8,2,25088]{2,1,0:T(2,128)(2,1)} %reshape.68), calls=%async_computation | async-start | bytes 1605632 | tf_op jit(solution)/shard_map/all_to_all | solution.py:56
  182.2 139.0 %all-gather.2.cloned.1.call-start = ((), (), s32[]{:S(2)}) async-start(), calls=%async_computation.2 | async-start | bytes 1806336 | tf_op jit(solution)/shard_map/all_gather | solution.py:65
  223.2 19.7 %copy-start.2 = (bf16[3,3,128,128]{3,2,1,0:T(8,128)(2,1)S(1)}, bf16[3,3,128,128]{3,2,1,0:T(8,128)(2,1)}, u32[]{:S(2)}) copy-start(bf16[3,3,128,128]{3,2,1,0:T(8,128)(2,1)} %param.10) | copy-start | bytes 884740
  242.9 81.6 %copy-start.1 = (bf16[3,3,1024,128]{3,2,1,0:T(8,128)(2,1)S(1)}, bf16[3,3,1024,128]{3,2,1,0:T(8,128)(2,1)}, u32[]{:S(2)}) copy-start(bf16[3,3,1024,128]{3,2,1,0:T(8,128)(2,1)} %param.11) | copy-start | bytes 7077892
  279.5 173.7 %all-reduce.10.cloned.1.call-start = ((), (), s32[]{:S(2)}) async-start(), calls=%async_computation.3 | async-start | bytes 401408
  341.8 0.7 copy-start.3
Sparse Core Ops, SparseCore 0:
  10.3 115.6 all-reduce.7
  279.6 41.5 all-gather.1
  342.6 110.6 all-reduce.9
where the time goes:
time: 463 us; the launch traced here: 462 us
  waiting for transfers between devices  289 us (62%)
  local copies, waits for them, and re-layouts  88.5 us (19%)
  blocking collectives  58.4 us (13%)
  between operations  13.3 us (3%)
  matrix products  6.06 us (1%)
    psum x1, waiting for transfers between devices, local(): summed = lax.psum(first_terms, 'cin')  117 us
    unnamed x4, waiting for transfers between devices  110 us
    all_gather x1, waiting for transfers between devices, local(): gathered = lax.all_gather(narrow, 'cout', axis=4, tiled=True)  41.6 us
    unnamed x19, local copies, waits for them, and re-layouts  36.8 us
    psum x1, blocking collectives, local(): summed_wide = lax.psum(reduced, 'img')  31.9 us
    all_gather x1, blocking collectives, local(): whole = lax.all_gather(segment_maps, 'cout', axis=4, tiled=True)  26.5 us
    all_to_all x1, waiting for transfers between devices, local(): lax.all_to_all(whole, 'img', split_axis=4, concat_axis=1, tiled=True)  21.2 us
    all_to_all x1, local copies, waits for them, and re-layouts, local(): lax.all_to_all(whole, 'img', split_axis=4, concat_axis=1, tiled=True)  17.3 us
  transfers between devices with their start and end apart: 4, of which 4 were waited for; matrix products, arithmetic and copies ran while one was open for 0% of the time, Pallas kernels for 0%

commit v1 on v0

--- a/solution.py
+++ b/solution.py
@@ -52,7 +52,9 @@
     summed = lax.psum(first_terms, "cin")
     own_part = lax.dynamic_slice_in_dim(maps, lax.axis_index("cout") * out_block, out_block, 4)
     segment_maps = (own_part.astype(jnp.float32) + summed).astype(jnp.bfloat16)
-    whole = lax.all_gather(segment_maps, "cout", axis=4, tiled=True)
+    whole = jnp.concatenate(
+        lax.all_to_all(jnp.stack([segment_maps] * lax.axis_size("cout")), "cout", 0, 0), axis=4
+    )
     by_channel = lax.all_to_all(whole, "img", split_axis=4, concat_axis=1, tiled=True)
     images = by_channel.shape[1]
     rect_segment = jnp.maximum(by_channel, 0).reshape(-1, side, side, by_channel.shape[4])

time: 463 us -> 458 us (0.989)
    all_gather x1 -> x0, blocking collectives: 26.5 us -> none  [local(): whole = lax.all_gather(segment_maps, 'cout', axis=4, tiled=True)]
    all_to_all x0 -> x1, blocking collectives: none -> 24.3 us  [local(): lax.all_to_all(jnp.stack([segment_maps] * lax.axis_size('cout')), 'cout',...]
    all_gather x1 -> x0, local copies, waits for them, and re-layouts: 12.4 us -> none  [local(): whole = lax.all_gather(segment_maps, 'cout', axis=4, tiled=True)]
    reshape x0 -> x1, local copies, waits for them, and re-layouts: none -> 12.3 us  [local(): jnp.concatenate(lax.all_to_all(jnp.stack([segment_maps] * lax.axis_size('...]
where the time goes in v1:
time: 458 us; the launch traced here: 457 us
  waiting for transfers between devices  286 us (62%)
  local copies, waits for them, and re-layouts  88.9 us (19%)
  blocking collectives  56.2 us (12%)
  between operations  13.3 us (3%)
  matrix products  6.06 us (1%)
    psum x1, waiting for transfers between devices, local(): summed = lax.psum(first_terms, 'cin')  117 us
    unnamed x4, waiting for transfers between devices  110 us
    all_gather x1, waiting for transfers between devices, local(): gathered = lax.all_gather(narrow, 'cout', axis=4, tiled=True)  38.5 us
    unnamed x19, local copies, waits for them, and re-layouts  36.8 us
    psum x1, blocking collectives, local(): summed_wide = lax.psum(reduced, 'img')  31.9 us
    all_to_all x1, blocking collectives, local(): lax.all_to_all(jnp.stack([segment_maps] * lax.axis_size('cout')), 'cout',...  24.3 us
    all_to_all x1, waiting for transfers between devices, local(): lax.all_to_all(whole, 'img', split_axis=4, concat_axis=1, tiled=True)  21.2 us
    all_to_all x1, local copies, waits for them, and re-layouts, local(): lax.all_to_all(whole, 'img', split_axis=4, concat_axis=1, tiled=True)  17.3 us
  transfers between devices with their start and end apart: 4, of which 4 were waited for; matrix products, arithmetic and copies ran while one was open for 0% of the time, Pallas kernels for 0%

profile of v1, /device:TPU:64, one launch (start us, length us, event | category | flops | bytes accessed | tf_op | source)
XLA Modules:
  0.0 456.9 jit_solution(2806415963040960365)
XLA Ops:
  9.3 116.6 %all-reduce.8.cloned.1.call-done = f32[2,1,14,14,128]{4,3,2,0,1:T(8,128)} async-done(((f32[2,1,14,14,128]{4,3,2,0,1:T(8,128)}), f32[2,1,14,14,128]{4,3,2,0,1:T(8,128)}) %all-reduce.8.cloned.1.call-update) | async-done | bytes 200720 | tf_op jit(solution)/shard_map/psum | solution.py:52
  127.5 24.3 %all_to_all.14 = bf16[8,2,1,14,14,128]{5,1,4,3,2,0:T(2,128)(2,1)S(1)} all-to-all(bf16[8,2,1,14,14,128]{5,1,4,3,2,0:T(2,128)(2,1)S(1)} %stack.2), channel_id=1, replica_groups=mesh['img'=8,'cin'=8,'cout'=8] {'cout'}, dimensions={0} | all-to-all | bytes 1605632 | tf_op jit(solution)/shard_map/all_to_all | solution.py:56
  151.7 12.3 %copy.60 = bf16[2,1,14,14,8,128]{3,0,2,5,4,1:T(2,128)(2,1)} copy(bf16[2,1,14,14,8,128]{5,0,3,2,1,4:T(2,128)(2,1)S(1)} %bitcast.92) | data formatting | bytes 1605632 | tf_op jit(solution)/shard_map/reshape | solution.py:55
  164.0 12.8 %reshape.79 = bf16[8,2,25088]{2,1,0:T(2,128)(2,1)} reshape(bf16[1024,1,14,2,14]{4,3,2,1,0:T(2,128)(2,1)} %bitcast.88) | data formatting | bytes 1605632
  176.9 3.5 all-to-all-start.1
  180.5 21.2 %all-to-all-done.1 = bf16[8,2,25088]{2,1,0:T(2,128)(2,1)S(1)} async-done(((bf16[8,2,25088]{2,1,0:T(2,128)(2,1)}), bf16[8,2,25088]{2,1,0:T(2,128)(2,1)S(1)}, u32[]{:S(2)}, u32[]{:S(2)}) %all-to-all-start.1) | async-done | bytes 802848 | tf_op jit(solution)/shard_map/all_to_all | solution.py:58
  201.6 19.8 %reshape.80 = bf16[1024,1,14,2,14]{4,3,2,1,0:T(2,128)(2,1)} reshape(bf16[8,2,25088]{2,1,0:T(2,128)(2,1)S(1)} %all-to-all-done.1) | data formatting | bytes 1605632
  221.4 17.3 %copy.49 = bf16[2,1,14,14,1024]{4,0,3,2,1:T(2,128)(2,1)S(1)} copy(bf16[2,1,14,14,1024]{3,0,2,1,4:T(2,128)(2,1)} %bitcast.89) | data formatting | bytes 1605632 | tf_op jit(solution)/shard_map/all_to_all | solution.py:58
  239.9 1.2 pad_bitcast_fusion.1
  241.1 4.0 while.26
  241.1 1.2 dynamic-slice_bitcast_fusion.6
  245.1 31.9 %all-reduce.11 = bf16[2,8,7,7,128]{4,1,0,3,2:T(8,128)(2,1)S(1)} all-reduce(f32[2,8,7,7,128]{4,1,0,3,2:T(8,128)S(1)} %get-tuple-element.61), channel_id=1, replica_groups=mesh['img'=8,'cin'=8,'cout'=8] {'img'}, use_global_device_ids=true, to_apply=%region_3.4 | all-reduce | flops 100352 | bytes 602112 | tf_op jit(solution)/shard_map/psum | solution.py:65
  278.0 38.5 %all-gather.2.cloned.1.call-done = bf16[2,8,7,7,1024]{4,1,0,3,2:T(8,128)(2,1)} async-done(((bf16[2,8,7,7,128]{4,1,0,3,2:T(8,128)(2,1)}), bf16[2,8,7,7,1024]{4,1,0,3,2:T(8,128)(2,1)}) %all-gather.2.cloned.1.call-update) | async-done | bytes 1605648 | tf_op jit(solution)/shard_map/all_gather | solution.py:67
  316.5 3.3 pad_bitcast_fusion
  319.8 17.2 %while.27 = (s32[]{:T(128)}, bf16[2,8,7,7,128]{4,0,3,2,1:T(2,128)(2,1)S(1)}, bf16[2,8,9,9,1024]{4,1,0,3,2:T(8,128)(2,1)}, bf16[9216,128]{1,0:T(8,128)(2,1)S(1)}) while((s32[]{:T(128)}, bf16[2,8,7,7,128]{4,0,3,2,1:T(2,128)(2,1)S(1)}, bf16[2,8,9,9,1024]{4,1,0,3,2:T(8,128)(2,1)}, bf16[9216,128]{1,0:T(8,128)(2,1)S(1)}) %tuple.60), condition=%wide.region_5.6_spmd.clone, body=%wide.region_4.5_spmd.sunk.clone | while | flops 924844032 | bytes 27191356 | solution.py:34
  319.8 1.4 dynamic-slice_bitcast_fusion.7
  321.8 2.0 fusion.30
  324.0 4.4 dynamic_update_slice.16
  328.4 1.4 dynamic-slice_bitcast_fusion.7
  330.4 2.0 fusion.30
  332.6 4.4 dynamic_update_slice.16
  337.7 1.3 dynamic-slice.2
  339.0 109.5 %all-reduce.10.cloned.1.call-done = bf16[2,8,7,7,128]{4,0,3,2,1:T(2,128)(2,1)} async-done(((bf16[2,8,7,7,128]{4,0,3,2,1:T(2,128)(2,1)}), bf16[2,8,7,7,128]{4,0,3,2,1:T(2,128)(2,1)}) %all-reduce.10.cloned.1.call-update) | async-done | bytes 200720
  448.5 1.9 constant_dynamic-slice_fusion
  (75 shorter events, 10.9 us)
Async XLA Ops:
  6.5 1.6 copy-start
  6.5 119.4 %all-reduce.8.cloned.1.call-start = ((), (), s32[]{:S(2)}) async-start(), calls=%async_computation.2 | async-start | bytes 458752 | tf_op jit(solution)/shard_map/psum | solution.py:52
  176.9 24.8 %all-to-all-start.1 = ((bf16[8,2,25088]{2,1,0:T(2,128)(2,1)}), bf16[8,2,25088]{2,1,0:T(2,128)(2,1)S(1)}, u32[]{:S(2)}, u32[]{:S(2)}) async-start(bf16[8,2,25088]{2,1,0:T(2,128)(2,1)} %reshape.79), calls=%async_computation.1 | async-start | bytes 1605632 | tf_op jit(solution)/shard_map/all_to_all | solution.py:58
  180.4 136.1 %all-gather.2.cloned.1.call-start = ((), (), s32[]{:S(2)}) async-start(), calls=%async_computation.3 | async-start | bytes 1806336 | tf_op jit(solution)/shard_map/all_gather | solution.py:67
  221.4 19.7 %copy-start.2 = (bf16[3,3,128,128]{3,2,1,0:T(8,128)(2,1)S(1)}, bf16[3,3,128,128]{3,2,1,0:T(8,128)(2,1)}, u32[]{:S(2)}) copy-start(bf16[3,3,128,128]{3,2,1,0:T(8,128)(2,1)} %param.10) | copy-start | bytes 884740
  241.1 78.7 %copy-start.1 = (bf16[3,3,1024,128]{3,2,1,0:T(8,128)(2,1)S(1)}, bf16[3,3,1024,128]{3,2,1,0:T(8,128)(2,1)}, u32[]{:S(2)}) copy-start(bf16[3,3,1024,128]{3,2,1,0:T(8,128)(2,1)} %param.11) | copy-start | bytes 7077892
  277.7 170.7 %all-reduce.10.cloned.1.call-start = ((), (), s32[]{:S(2)}) async-start(), calls=%async_computation.4 | async-start | bytes 401408
  337.0 0.7 copy-start.3
Sparse Core Ops, SparseCore 0:
  10.3 115.6 all-reduce.7
  277.9 38.5 all-gather.1
  337.8 110.6 all-reduce.9
